TPU v7x, 128 devices: a whole 4x4x4 slice. The times are simulated.
128 devices in a mesh: samp: 32 (over x, y, core), var: 4 (over z).
Axes of the slice: x: 4, y: 4, z: 4, core: 2. Of those that a mesh axis runs over, the one named last changes fastest.
Arguments:
- genotypes: int32 [32768, 4096], P('samp', 'var'), may hold values from 0 to 2
- observed: int32 [32768, 4096], P('samp', 'var'), may hold values from 0 to 1, as said below
- proportions: float32 [10, 32768], P(None, 'samp'), may hold values from 0 to 1, as said below
- frequencies: float32 [10, 4096], P(None, ('samp', 'var')), may hold values from 0.02 to 0.98
Outputs:
- mixture: float32 [10, 32768], P(None, 'samp')
- alleles: float32 [10, 4096], P(None, 'var')
Inputs may be any that keep to these rules, and one draw needn't show every extreme that they name: Every sample is observed at 256 or more variants and every variant at 2048 or more samples. Each sample's 10 proportions are positive and sum to one.
All inputs are finite; a program needn't handle non-finite values.
Results may differ from a plain program's by a relative error of at most 0.0003.
Values sent between devices are 32-bit elements; how exact they have to be, the bound alone decides.
A program may use at most 128 MiB of HBM per device.

v0:
```python
import jax
import jax.numpy as jnp
from jax import lax
from jax.sharding import PartitionSpec as P

STEPS = 2
CLIP_LOW = 1e-05
NORM_EPS = 1e-10
EXACT = lax.Precision.HIGHEST


def clip_unit(values):
    return jnp.clip(values, CLIP_LOW, 1.0 - CLIP_LOW)


def tidy_mixture(mixture):
    clipped = clip_unit(mixture)
    return clipped / jnp.sum(clipped, axis=0, keepdims=True)


def step_size(first, second):
    return jnp.maximum(1.0, jnp.sqrt(first / (second + NORM_EPS)))


def allele_rule(alleles, alt_sums, ref_sums):
    weighted = alleles * alt_sums
    return clip_unit(weighted / (weighted + (1.0 - alleles) * ref_sums))


def local(genotypes, observed, proportions, frequencies):
    var_count = lax.axis_size("var")
    gathered = lax.all_gather(frequencies, ("samp", "var"), axis=1, tiled=True)
    owner_width = gathered.shape[1] // var_count
    alleles = lax.dynamic_slice_in_dim(
        gathered, lax.axis_index("var") * owner_width, owner_width, 1
    )
    seen_vals = observed.astype(jnp.float32)
    geno_vals = genotypes.astype(jnp.float32)
    alt_counts = seen_vals * geno_vals
    ref_counts = seen_vals * (2.0 - geno_vals)
    local_counts = jnp.sum(observed, axis=1).astype(jnp.float32)
    twice_observed = 2.0 * lax.psum(local_counts, "var")[None, :]

    def expectation_step(mixture, current):
        expected = lax.dot_general(
            mixture,
            current,
            (((0,), (0,)), ((), ())),
            precision=EXACT,
            preferred_element_type=jnp.float32,
        )
        ratio_alt = alt_counts / expected
        ratio_ref = ref_counts / (1.0 - expected)
        prop_terms = lax.dot_general(
            current,
            ratio_alt - ratio_ref,
            (((1,), (1,)), ((), ())),
            precision=EXACT,
            preferred_element_type=jnp.float32,
        )
        prop_terms = prop_terms + jnp.sum(ratio_ref, axis=1)[None, :]
        alt_terms = lax.dot_general(
            mixture,
            ratio_alt,
            (((1,), (0,)), ((), ())),
            precision=EXACT,
            preferred_element_type=jnp.float32,
        )
        ref_terms = lax.dot_general(
            mixture,
            ratio_ref,
            (((1,), (0,)), ((), ())),
            precision=EXACT,
            preferred_element_type=jnp.float32,
        )
        prop_sums = lax.psum(prop_terms, "var")
        next_mixture = clip_unit(mixture * prop_sums / twice_observed)
        alt_sums, ref_sums = lax.psum((alt_terms, ref_terms), "samp")
        next_alleles = allele_rule(current, alt_sums, ref_sums)
        return (next_mixture, next_alleles)

    mixture = proportions
    for repeat in range(STEPS):
        mixture_one, alleles_one = expectation_step(mixture, alleles)
        mixture_two, alleles_two = expectation_step(mixture_one, alleles_one)
        step_mix = mixture_one - mixture
        curve_mix = mixture_two - mixture_one - step_mix
        step_allele = alleles_one - alleles
        curve_allele = alleles_two - alleles_one - step_allele
        step_mix_local = jnp.sum(step_mix * step_mix)
        curve_mix_local = jnp.sum(curve_mix * curve_mix)
        step_allele_local = jnp.sum(step_allele * step_allele)
        curve_allele_local = jnp.sum(curve_allele * curve_allele)
        step_allele_sum, curve_allele_sum = lax.psum((step_allele_local, curve_allele_local), "var")
        step_mix_sum, curve_mix_sum = lax.psum((step_mix_local, curve_mix_local), "samp")
        alpha_mix = step_size(step_mix_sum, curve_mix_sum)
        alpha_allele = step_size(step_allele_sum, curve_allele_sum)
        extra_mix = tidy_mixture(
            mixture + 2.0 * alpha_mix * step_mix + alpha_mix * alpha_mix * curve_mix
        )
        extra_allele = clip_unit(
            alleles + 2.0 * alpha_allele * step_allele + alpha_allele * alpha_allele * curve_allele
        )
        mixture, alleles = expectation_step(extra_mix, extra_allele)
    return (mixture, alleles)


def solution(mesh):
    placed = (P("samp", "var"), P("samp", "var"), P(None, "samp"), P(None, ("samp", "var")))
    return jax.shard_map(
        local,
        mesh=mesh,
        in_specs=placed,
        out_specs=(P(None, "samp"), P(None, "var")),
        check_vma=False,
    )
```

profile of v0, /device:TPU:1, one launch (start us, length us, event | category | flops | bytes accessed | tf_op | source)
XLA Modules:
  0.0 985.0 jit_solution(3233084332891088129)
XLA Ops:
  7.2 64.1 %all-gather = f32[128,32,10]{1,2,0:T(8,128)S(1)} all-gather(f32[1,32,10]{1,2,0:T(8,128)} %bitcast.70), channel_id=1, replica_groups=mesh['samp'=32,'var'=4] {'samp','var'}, dimensions={0}, use_global_device_ids=true | all-gather | bytes 165120 | tf_op jit(solution)/shard_map/all_gather | solution.py:32
  71.8 5.4 copy.14
  77.2 5.4 copy.13
  82.6 12.0 %fusion.78 = (f32[1024]{0:T(1024)S(1)}, f32[1024,1024]{0,1:T(8,128)S(1)}, f32[1024,1024]{0,1:T(8,128)}, f32[1024,1024]{0,1:T(8,128)S(1)}, f32[1024,1024]{1,0:T(8,128)S(1)}) fusion(s32[1024,1024]{0,1:T(8,128)} %copy.14, s32[1024,1024]{0,1:T(8,128)} %copy.13, f32[10,1024]{1,0:T(8,128)S(1)} %copy-done.11, f32[4096,10]{0,1:T(8,128)S(1)} %reshape.15, ...), kind=kOutput, calls=%fused_computation.104 | convolution fusion | flops 134216704 | bytes 25300996 | tf_op jit(solution)/shard_map/dot_general | solution.py:45
  94.6 2.0 copy-done
  96.5 4.3 convolution_bitcast_fusion
  100.8 4.7 convolution_bitcast_fusion.1
  105.5 10.7 %all-reduce.20.cloned.1.call-start = ((), (), s32[]{:S(2)}) async-start(), calls=%async_computation.2 | async-start | bytes 262144 | tf_op jit(solution)/shard_map/psum | solution.py:78
  116.2 2.5 reduce_sum.154
  118.6 7.4 fusion.13
  126.0 13.1 %all-reduce.8 = (f32[10,1024]{1,0:T(8,128)S(1)}, f32[1024]{0:T(1024)S(1)}) all-reduce(f32[10,1024]{1,0:T(8,128)S(1)} %fusion.13, f32[1024]{0:T(1024)S(1)} %convert_element_type.11), channel_id=1, replica_groups=mesh['samp'=32,'var'=4] {'var'}, use_global_device_ids=true, to_apply=%region_1.0 | all-reduce | flops 11264 | bytes 90112 | tf_op jit(solution)/shard_map/psum | solution.py:76
  139.2 65.9 %all-reduce.22.cloned.1.call-done = (f32[10,1024]{1,0:T(8,128)}, f32[10,1024]{1,0:T(8,128)}) async-done(((f32[10,1024]{1,0:T(8,128)}, f32[10,1024]{1,0:T(8,128)}), (f32[10,1024]{1,0:T(8,128)}, f32[10,1024]{1,0:T(8,128)})) %all-reduce.22.cloned.1.call-update) | async-done | bytes 81936 | tf_op jit(solution)/shard_map/psum | solution.py:78
  205.1 1.5 multiply_reduce_fusion.5
  206.6 9.0 fusion.77
  215.6 3.5 fusion.65
  219.2 3.5 fusion.80
  222.7 2.7 fusion.16
  225.4 14.0 %psum.194 = f32[10,1024]{1,0:T(8,128)S(1)} all-reduce(f32[10,1024]{1,0:T(8,128)S(1)} %fusion.16), channel_id=1, replica_groups=mesh['samp'=32,'var'=4] {'var'}, use_global_device_ids=true, to_apply=%region_9.10 | all-reduce | flops 10240 | bytes 81920 | tf_op jit(solution)/shard_map/psum | solution.py:76
  240.0 125.1 %all-reduce.23 = (f32[10,1024]{1,0:T(8,128)S(1)}, f32[10,1024]{1,0:T(8,128)S(1)}, f32[]{:T(128)}, f32[]{:T(128)}) all-reduce(f32[10,1024]{1,0:T(8,128)S(1)} %fusion.80, f32[10,1024]{1,0:T(8,128)S(1)} %fusion.65, f32[]{:T(128)} %get-tuple-element.5, f32[]{:T(128)} %get-tuple-element.4), channel_id=1, replica_groups=mesh['samp'=32,'var'=4] {'samp'}, use_global_device_ids=true, to_apply=%region_16.17 | all-reduce | flops 20482 | bytes 163856 | tf_op jit(solution)/shard_map/psum | solution.py:78
  367.0 7.0 all-reduce.7
  375.5 9.0 fusion.73
  384.5 4.2 fusion.50
  388.7 4.2 fusion.49
  392.9 7.3 fusion.19
  400.3 12.7 %psum.200 = f32[10,1024]{1,0:T(8,128)S(1)} all-reduce(f32[10,1024]{1,0:T(8,128)S(1)} %fusion.19), channel_id=1, replica_groups=mesh['samp'=32,'var'=4] {'var'}, use_global_device_ids=true, to_apply=%region_20.21 | all-reduce | flops 10240 | bytes 81920 | tf_op jit(solution)/shard_map/psum | solution.py:76
  413.3 106.5 %all-reduce.20.cloned.1.call-done = (f32[10,1024]{1,0:T(8,128)}, f32[10,1024]{1,0:T(8,128)}) async-done(((f32[10,1024]{1,0:T(8,128)}, f32[10,1024]{1,0:T(8,128)}), (f32[10,1024]{1,0:T(8,128)}, f32[10,1024]{1,0:T(8,128)})) %all-reduce.20.cloned.1.call-update) | async-done | bytes 81936 | tf_op jit(solution)/shard_map/psum | solution.py:78
  519.8 0.9 fusion.35
  520.7 9.0 fusion.72
  529.7 4.2 fusion.60
  533.9 4.2 fusion.81
  538.1 7.3 fusion.22
  545.4 13.9 %psum.203 = f32[10,1024]{1,0:T(8,128)S(1)} all-reduce(f32[10,1024]{1,0:T(8,128)S(1)} %fusion.22), channel_id=1, replica_groups=mesh['samp'=32,'var'=4] {'var'}, use_global_device_ids=true, to_apply=%region_24.25 | all-reduce | flops 10240 | bytes 81920 | tf_op jit(solution)/shard_map/psum | solution.py:76
  559.7 102.3 %all-reduce.18.cloned.1.call-done = (f32[10,1024]{1,0:T(8,128)}, f32[10,1024]{1,0:T(8,128)}) async-done(((f32[10,1024]{1,0:T(8,128)}, f32[10,1024]{1,0:T(8,128)}), (f32[10,1024]{1,0:T(8,128)}, f32[10,1024]{1,0:T(8,128)})) %all-reduce.18.cloned.1.call-update) | async-done | bytes 81936 | tf_op jit(solution)/shard_map/psum | solution.py:78
  662.1 0.9 fusion.36
  663.0 9.0 fusion.71
  672.0 3.5 fusion.57
  675.5 3.5 fusion.82
  679.1 2.7 fusion.25
  681.7 13.9 %psum.207 = f32[10,1024]{1,0:T(8,128)S(1)} all-reduce(f32[10,1024]{1,0:T(8,128)S(1)} %fusion.25), channel_id=1, replica_groups=mesh['samp'=32,'var'=4] {'var'}, use_global_device_ids=true, to_apply=%region_30.31 | all-reduce | flops 10240 | bytes 81920 | tf_op jit(solution)/shard_map/psum | solution.py:76
  696.3 125.1 %all-reduce.24 = (f32[10,1024]{1,0:T(8,128)S(1)}, f32[10,1024]{1,0:T(8,128)S(1)}, f32[]{:T(128)}, f32[]{:T(128)}) all-reduce(f32[10,1024]{1,0:T(8,128)S(1)} %fusion.82, f32[10,1024]{1,0:T(8,128)S(1)} %fusion.57, f32[]{:T(128)} %get-tuple-element.3, f32[]{:T(128)} %get-tuple-element.2), channel_id=1, replica_groups=mesh['samp'=32,'var'=4] {'samp'}, use_global_device_ids=true, to_apply=%region_37.38 | all-reduce | flops 20482 | bytes 163856 | tf_op jit(solution)/shard_map/psum | solution.py:78
  824.0 6.9 all-reduce.6
  832.3 9.0 fusion.68
  841.4 4.2 fusion.53
  845.6 4.2 fusion.52
  849.8 7.3 fusion.28
  857.1 12.7 %psum.213 = f32[10,1024]{1,0:T(8,128)S(1)} all-reduce(f32[10,1024]{1,0:T(8,128)S(1)} %fusion.28), channel_id=1, replica_groups=mesh['samp'=32,'var'=4] {'var'}, use_global_device_ids=true, to_apply=%region_41.42 | all-reduce | flops 10240 | bytes 81920 | tf_op jit(solution)/shard_map/psum | solution.py:76
  870.5 106.0 %all-reduce.16.cloned.1.call-done = (f32[10,1024]{1,0:T(8,128)}, f32[10,1024]{1,0:T(8,128)}) async-done(((f32[10,1024]{1,0:T(8,128)}, f32[10,1024]{1,0:T(8,128)}), (f32[10,1024]{1,0:T(8,128)}, f32[10,1024]{1,0:T(8,128)})) %all-reduce.16.cloned.1.call-update) | async-done | bytes 81936 | tf_op jit(solution)/shard_map/psum | solution.py:78
  976.5 1.5 fusion.40
  (52 shorter events, 5.2 us)
Async XLA Ops:
  7.2 197.9 %all-reduce.22.cloned.1.call-start = ((), (), s32[]{:S(2)}) async-start(), calls=%async_computation.3 | async-start | bytes 262144 | tf_op jit(solution)/shard_map/psum | solution.py:78
  77.2 5.4 copy-start.11
  94.6 2.0 copy-start
  94.6 6.2 copy-start.4
  94.6 6.2 copy-start.10
  105.5 414.3 %all-reduce.20.cloned.1.call-start = ((), (), s32[]{:S(2)}) async-start(), calls=%async_computation.2 | async-start | bytes 262144 | tf_op jit(solution)/shard_map/psum | solution.py:78
  206.6 9.0 copy-start.5
  375.5 9.1 copy-start.6
  384.5 4.2 copy-start.13
  384.5 4.2 copy-start.2
  413.0 249.0 %all-reduce.18.cloned.1.call-start = ((), (), s32[]{:S(2)}) async-start(), calls=%async_computation.1 | async-start | bytes 262144 | tf_op jit(solution)/shard_map/psum | solution.py:78
  520.7 9.1 copy-start.7
  529.7 4.2 copy-start.14
  529.7 4.2 copy-start.3
  559.4 417.1 %all-reduce.16.cloned.1.call-start = ((), (), s32[]{:S(2)}) async-start(), calls=%async_computation | async-start | bytes 262144 | tf_op jit(solution)/shard_map/psum | solution.py:78
  663.0 9.0 copy-start.8
  832.3 9.1 copy-start.9
  841.4 4.2 copy-start.12
  841.4 4.2 copy-start.1
Sparse Core Ops, SparseCore 0:
  105.6 99.4 all-reduce.21
  413.2 106.5 all-reduce.19
  559.5 102.4 all-reduce.17
  870.0 106.4 all-reduce.15
where the time goes:
time: 994 us; the launch traced here: 985 us
  blocking collectives  409 us (41%)
  waiting for transfers between devices  381 us (38%)
  matrix products  140 us (14%)
  between operations  19.9 us (2%)
  local copies, waits for them, and re-layouts  13.3 us (1%)
  other arithmetic  11.3 us (1%)
  starting transfers between devices  11.2 us (1%)
    psum x4, waiting for transfers between devices, expectation_step(): alt_sums, ref_sums = lax.psum((alt_terms, ref_terms), 'samp')  381 us
    psum x2, blocking collectives, expectation_step(): alt_sums, ref_sums = lax.psum((alt_terms, ref_terms), 'samp')  250 us
    psum x6, blocking collectives, expectation_step(): prop_sums = lax.psum(prop_terms, 'var')  80.4 us
    all_gather x1, blocking collectives, local(): gathered = lax.all_gather(frequencies, ('samp', 'var'), axis=1, tiled=True)  64.1 us
    dot_general x6, matrix products, expectation_step(): lax.dot_general(mixture, current, (((0,), (0,)), ((), ())), precision=EXA...  57.1 us
    dot_general x6, matrix products, expectation_step(): lax.dot_general(current, ratio_alt - ratio_ref, (((1,), (1,)), ((), ())),...  34.7 us
    dot_general x6, matrix products, expectation_step(): lax.dot_general(mixture, ratio_alt, (((1,), (0,)), ((), ())), precision=E...  24.2 us
    dot_general x6, matrix products, expectation_step(): lax.dot_general(mixture, ratio_ref, (((1,), (0,)), ((), ())), precision=E...  24 us
  transfers between devices with their start and end apart: 4, of which 4 were waited for; matrix products, arithmetic and copies ran while one was open for 1% of the time, Pallas kernels for 0%

commit v1 on v0

--- a/solution.py
+++ b/solution.py
@@ -73,7 +73,11 @@
             precision=EXACT,
             preferred_element_type=jnp.float32,
         )
-        prop_sums = lax.psum(prop_terms, "var")
+        prop_sums = prop_terms
+        for hop in (1, 2):
+            prop_sums = prop_sums + lax.ppermute(
+                prop_sums, "var", [(dev, dev ^ hop) for dev in range(4)]
+            )
         next_mixture = clip_unit(mixture * prop_sums / twice_observed)
         alt_sums, ref_sums = lax.psum((alt_terms, ref_terms), "samp")
         next_alleles = allele_rule(current, alt_sums, ref_sums)

time: 994 us -> 917 us (0.923)
  blocking collectives: 409 us -> 335 us
  matrix products: 140 us -> 121 us
  waiting for transfers between devices: 381 us -> 391 us
    psum x6 -> x1, blocking collectives: 80.4 us -> 7.45 us  [local(): twice_observed = 2.0 * lax.psum(local_counts, 'var')[None, :]]
    dot_general x6, matrix products: 34.7 us -> 16 us  [expectation_step(): lax.dot_general(current, ratio_alt - ratio_ref, (((1,), (1,)), ((), ())),...]
    ppermute x0 -> x12, starting transfers between devices: none -> 18.4 us  [expectation_step(): lax.ppermute(prop_sums, 'var', [(dev, dev ^ hop) for dev in range(4)])]
    psum x4, starting transfers between devices: 11.2 us -> 0.16 us  [expectation_step(): alt_sums, ref_sums = lax.psum((alt_terms, ref_terms), 'samp')]
    psum x4, waiting for transfers between devices: 381 us -> 391 us  [expectation_step(): alt_sums, ref_sums = lax.psum((alt_terms, ref_terms), 'samp')]
  transfers between devices with their start and end apart: 4 -> 16, of which waited for: 4 -> 4; matrix products, arithmetic and copies ran while one was open for 1% -> 5% of each run, Pallas kernels for 0% -> 0%
where the time goes in v1:
time: 917 us; the launch traced here: 910 us
  waiting for transfers between devices  391 us (43%)
  blocking collectives  335 us (37%)
  matrix products  121 us (13%)
  between operations  19.7 us (2%)
  starting transfers between devices  18.5 us (2%)
  other arithmetic  12.6 us (1%)
  local copies, waits for them, and re-layouts  11.3 us (1%)
    psum x4, waiting for transfers between devices, expectation_step(): alt_sums, ref_sums = lax.psum((alt_terms, ref_terms), 'samp')  391 us
    psum x2, blocking collectives, expectation_step(): alt_sums, ref_sums = lax.psum((alt_terms, ref_terms), 'samp')  249 us
    all_gather x1, blocking collectives, local(): gathered = lax.all_gather(frequencies, ('samp', 'var'), axis=1, tiled=True)  64.1 us
    dot_general x6, matrix products, expectation_step(): lax.dot_general(mixture, current, (((0,), (0,)), ((), ())), precision=EXA...  57.1 us
    dot_general x6, matrix products, expectation_step(): lax.dot_general(mixture, ratio_alt, (((1,), (0,)), ((), ())), precision=E...  24.2 us
    dot_general x6, matrix products, expectation_step(): lax.dot_general(mixture, ratio_ref, (((1,), (0,)), ((), ())), precision=E...  23.8 us
    ppermute x12, starting transfers between devices, expectation_step(): lax.ppermute(prop_sums, 'var', [(dev, dev ^ hop) for dev in range(4)])  18.4 us
  transfers between devices with their start and end apart: 16, of which 4 were waited for; matrix products, arithmetic and copies ran while one was open for 5% of the time, Pallas kernels for 0%

profile of v1, /device:TPU:1, one launch (start us, length us, event | category | flops | bytes accessed | tf_op | source)
XLA Modules:
  0.0 909.6 jit_solution(1540331181360101507)
XLA Ops:
  7.2 64.1 %all-gather = f32[128,32,10]{1,2,0:T(8,128)S(1)} all-gather(f32[1,32,10]{1,2,0:T(8,128)} %bitcast.70), channel_id=1, replica_groups=mesh['samp'=32,'var'=4] {'samp','var'}, dimensions={0}, use_global_device_ids=true | all-gather | bytes 165120 | tf_op jit(solution)/shard_map/all_gather | solution.py:32
  71.8 5.3 copy.14
  77.2 5.4 copy.13
  82.6 12.0 %fusion.78 = (f32[1024]{0:T(1024)S(1)}, f32[1024,1024]{0,1:T(8,128)S(1)}, f32[1024,1024]{0,1:T(8,128)}, f32[1024,1024]{0,1:T(8,128)S(1)}, f32[1024,1024]{1,0:T(8,128)S(1)}) fusion(s32[1024,1024]{0,1:T(8,128)} %copy.14, s32[1024,1024]{0,1:T(8,128)} %copy.13, f32[10,1024]{1,0:T(8,128)S(1)} %copy-done.6, f32[4096,10]{0,1:T(8,128)S(1)} %reshape.15, ...), kind=kOutput, calls=%fused_computation.104 | convolution fusion | flops 134216704 | bytes 25300996 | tf_op jit(solution)/shard_map/dot_general | solution.py:45
  94.6 2.7 fusion.13
  97.7 4.7 convolution_bitcast_fusion.1
  102.4 4.3 convolution_bitcast_fusion
  106.7 2.5 reduce_sum.154
  109.2 7.4 psum.147
  117.3 90.2 %all-reduce.21.cloned.1.call-done = (f32[10,1024]{1,0:T(8,128)}, f32[10,1024]{1,0:T(8,128)}) async-done(((f32[10,1024]{1,0:T(8,128)}, f32[10,1024]{1,0:T(8,128)}), (f32[10,1024]{1,0:T(8,128)}, f32[10,1024]{1,0:T(8,128)})) %all-reduce.21.cloned.1.call-update) | async-done | bytes 81936 | tf_op jit(solution)/shard_map/psum | solution.py:82
  207.5 1.5 multiply_reduce_fusion.5
  209.1 9.0 fusion.77
  218.1 2.7 fusion.16
  220.8 1.4 collective-permute-start.2
  222.2 3.5 fusion.65
  225.8 2.7 collective-permute-start.3
  228.4 3.5 fusion.80
  233.2 124.6 %all-reduce.22 = (f32[10,1024]{1,0:T(8,128)S(1)}, f32[10,1024]{1,0:T(8,128)S(1)}, f32[]{:T(128)}, f32[]{:T(128)}) all-reduce(f32[10,1024]{1,0:T(8,128)S(1)} %fusion.80, f32[10,1024]{1,0:T(8,128)S(1)} %fusion.65, f32[]{:T(128)} %multiply_reduce_fusion.7, f32[]{:T(128)} %get-tuple-element.44), channel_id=1, replica_groups=mesh['samp'=32,'var'=4] {'samp'}, use_global_device_ids=true, to_apply=%region_14.15 | all-reduce | flops 20482 | bytes 163856 | tf_op jit(solution)/shard_map/psum | solution.py:82
  359.7 7.2 all-reduce.7
  368.4 9.0 fusion.73
  377.4 4.2 fusion.50
  381.6 2.7 fusion.19
  384.2 1.1 collective-permute-start.4
  385.3 4.2 fusion.49
  389.6 1.7 collective-permute-start.5
  391.2 101.5 %all-reduce.19.cloned.1.call-done = (f32[10,1024]{1,0:T(8,128)}, f32[10,1024]{1,0:T(8,128)}) async-done(((f32[10,1024]{1,0:T(8,128)}, f32[10,1024]{1,0:T(8,128)}), (f32[10,1024]{1,0:T(8,128)}, f32[10,1024]{1,0:T(8,128)})) %all-reduce.19.cloned.1.call-update) | async-done | bytes 81936 | tf_op jit(solution)/shard_map/psum | solution.py:82
  493.7 9.0 fusion.72
  502.8 4.2 fusion.60
  506.9 2.7 fusion.22
  509.6 1.3 collective-permute-start.6
  510.9 4.2 fusion.81
  515.2 2.8 collective-permute-start.7
  518.0 97.6 %all-reduce.17.cloned.1.call-done = (f32[10,1024]{1,0:T(8,128)}, f32[10,1024]{1,0:T(8,128)}) async-done(((f32[10,1024]{1,0:T(8,128)}, f32[10,1024]{1,0:T(8,128)}), (f32[10,1024]{1,0:T(8,128)}, f32[10,1024]{1,0:T(8,128)})) %all-reduce.17.cloned.1.call-update) | async-done | bytes 81936 | tf_op jit(solution)/shard_map/psum | solution.py:82
  616.5 9.0 fusion.71
  625.5 2.7 fusion.25
  628.2 1.3 collective-permute-start.8
  629.5 3.5 fusion.57
  633.0 2.7 collective-permute-start.9
  635.7 3.5 fusion.82
  640.5 124.7 %all-reduce.23 = (f32[10,1024]{1,0:T(8,128)S(1)}, f32[10,1024]{1,0:T(8,128)S(1)}, f32[]{:T(128)}, f32[]{:T(128)}) all-reduce(f32[10,1024]{1,0:T(8,128)S(1)} %fusion.82, f32[10,1024]{1,0:T(8,128)S(1)} %fusion.57, f32[]{:T(128)} %multiply_reduce_fusion.3, f32[]{:T(128)} %get-tuple-element.29), channel_id=1, replica_groups=mesh['samp'=32,'var'=4] {'samp'}, use_global_device_ids=true, to_apply=%region_32.33 | all-reduce | flops 20482 | bytes 163856 | tf_op jit(solution)/shard_map/psum | solution.py:82
  767.7 7.2 all-reduce.6
  776.4 9.0 fusion.68
  785.4 4.2 fusion.53
  789.6 2.7 fusion.28
  793.3 4.2 fusion.52
  797.5 1.3 collective-permute-start.11
  798.8 101.9 %all-reduce.15.cloned.1.call-done = (f32[10,1024]{1,0:T(8,128)}, f32[10,1024]{1,0:T(8,128)}) async-done(((f32[10,1024]{1,0:T(8,128)}, f32[10,1024]{1,0:T(8,128)}), (f32[10,1024]{1,0:T(8,128)}, f32[10,1024]{1,0:T(8,128)})) %all-reduce.15.cloned.1.call-update) | async-done | bytes 81936 | tf_op jit(solution)/shard_map/psum | solution.py:82
  900.7 1.5 fusion.40
  (63 shorter events, 10.1 us)
Async XLA Ops:
  7.2 200.4 %all-reduce.21.cloned.1.call-start = ((), (), s32[]{:S(2)}) async-start(), calls=%async_computation.3 | async-start | bytes 262144 | tf_op jit(solution)/shard_map/psum | solution.py:82
  77.2 5.4 copy-start.6
  94.6 3.1 copy-start
  97.2 19.4 %collective-permute-start = (f32[10,1024]{1,0:T(8,128)S(1)}, f32[10,1024]{1,0:T(8,128)S(1)}, u32[]{:S(2)}, u32[]{:S(2)}) collective-permute-start(f32[10,1024]{1,0:T(8,128)S(1)} %fusion.13), channel_id=1, source_target_pairs={{0,1},{1,0},{2,3},{3,2},{4,5},{5,4},{6,7},{7,6},{8,9},{9,8},{10,11... | collective-permute-start | bytes 122888 | tf_op jit(solution)/shard_map/ppermute | solution.py:78
  106.6 386.1 %all-reduce.19.cloned.1.call-start = ((), (), s32[]{:S(2)}) async-start(), calls=%async_computation.2 | async-start | bytes 262144 | tf_op jit(solution)/shard_map/psum | solution.py:82
  116.6 92.4 %collective-permute-start.1 = (f32[10,1024]{1,0:T(8,128)S(1)}, f32[10,1024]{1,0:T(8,128)S(1)}, u32[]{:S(2)}, u32[]{:S(2)}) collective-permute-start(f32[10,1024]{1,0:T(8,128)S(1)} %add.186), channel_id=1, source_target_pairs={{0,2},{1,3},{2,0},{3,1},{4,6},{5,7},{6,4},{7,5},{8,10},{9,11},{10,... | collective-permute-start | bytes 122888 | tf_op jit(solution)/shard_map/ppermute | solution.py:78
  209.1 9.0 copy-start.1
  220.8 5.0 collective-permute-start.2
  225.8 6.2 collective-permute-start.3
  368.3 9.0 copy-start.2
  384.2 5.3 collective-permute-start.4
  389.5 226.0 %all-reduce.17.cloned.1.call-start = ((), (), s32[]{:S(2)}) async-start(), calls=%async_computation.1 | async-start | bytes 262144 | tf_op jit(solution)/shard_map/psum | solution.py:82
  389.6 104.1 %collective-permute-start.5 = (f32[10,1024]{1,0:T(8,128)S(1)}, f32[10,1024]{1,0:T(8,128)S(1)}, u32[]{:S(2)}, u32[]{:S(2)}) collective-permute-start(f32[10,1024]{1,0:T(8,128)S(1)} %add.202), channel_id=1, source_target_pairs={{0,2},{1,3},{2,0},{3,1},{4,6},{5,7},{6,4},{7,5},{8,10},{9,11},{10,... | collective-permute-start | bytes 122888 | tf_op jit(solution)/shard_map/ppermute | solution.py:78
  493.7 9.0 copy-start.3
  509.6 5.5 collective-permute-start.6
  515.1 385.6 %all-reduce.15.cloned.1.call-start = ((), (), s32[]{:S(2)}) async-start(), calls=%async_computation | async-start | bytes 262144 | tf_op jit(solution)/shard_map/psum | solution.py:82
  515.2 101.3 %collective-permute-start.7 = (f32[10,1024]{1,0:T(8,128)S(1)}, f32[10,1024]{1,0:T(8,128)S(1)}, u32[]{:S(2)}, u32[]{:S(2)}) collective-permute-start(f32[10,1024]{1,0:T(8,128)S(1)} %add.207), channel_id=1, source_target_pairs={{0,2},{1,3},{2,0},{3,1},{4,6},{5,7},{6,4},{7,5},{8,10},{9,11},{10,... | collective-permute-start | bytes 122888 | tf_op jit(solution)/shard_map/ppermute | solution.py:78
  616.5 9.0 copy-start.4
  628.2 4.8 collective-permute-start.8
  633.0 6.2 collective-permute-start.9
  776.3 9.0 copy-start.5
  792.2 5.3 collective-permute-start.10
  797.5 104.7 %collective-permute-start.11 = (f32[10,1024]{1,0:T(8,128)S(1)}, f32[10,1024]{1,0:T(8,128)S(1)}, u32[]{:S(2)}, u32[]{:S(2)}) collective-permute-start(f32[10,1024]{1,0:T(8,128)S(1)} %add.223), channel_id=1, source_target_pairs={{0,2},{1,3},{2,0},{3,1},{4,6},{5,7},{6,4},{7,5},{8,10},{9,11},{10,... | collective-permute-start | bytes 122888 | tf_op jit(solution)/shard_map/ppermute | solution.py:78
Sparse Core Ops, SparseCore 0:
  106.8 100.7 all-reduce.20
  389.6 103.1 all-reduce.18
  515.2 100.2 all-reduce.16
  797.6 103.0 all-reduce.14
